TPU v7x, 128 devices: a whole 4x4x4 slice. The times are simulated.
128 devices in a mesh: section: 2 (over core), dp: 16 (over y, x), tensor: 4 (over z).
Axes of the slice: x: 4, y: 4, z: 4, core: 2. Of those that a mesh axis runs over, the one named last changes fastest.
Arguments:
- layer_input: bfloat16 [2, 4096, 2, 4096], P('section', 'dp', None, 'tensor'), may hold values from -60 to 60
- norm_gain: float32 [2, 4096], P('section'), may hold values from 0.5 to 1.5
- upstream_grad: bfloat16 [2, 4096, 2, 4096], P('section', 'dp', None, 'tensor'), may hold values from -80 to 80
- saved_queries: bfloat16 [2, 4096, 2, 2048], P('section', 'dp', None, 'tensor'), may hold values from -150 to 150
- saved_keys: bfloat16 [2, 4096, 2, 1024], P('section', 'dp', None, 'tensor'), may hold values from -5 to 5
- saved_values: bfloat16 [2, 4096, 2, 1024], P('section', 'dp', None, 'tensor'), may hold values from -6 to 6
- segment_ids: int32 [2, 2, 4096], P('section', None, 'dp'), may hold values from 0 to 63, never falling along the last dimension, each value on 1 to 128 neighbouring positions
- batch_order: int32 [2, 16, 2], P('section', 'dp'), may hold values from 0 to 1, each once within a row
- qkv_weight: bfloat16 [2, 4096, 4096], P('section', None, 'tensor'), may hold values from -0.09375 to 0.09375
- out_weight: bfloat16 [2, 2048, 4096], P('section', 'tensor'), may hold values from -0.125 to 0.125
Outputs:
- passed_grad: bfloat16 [2, 4096, 2, 4096], P('section', 'dp', None, 'tensor')
- qkv_grad: float32 [2, 4096, 4096], P('section', 'dp', 'tensor')
- out_grad: float32 [2, 2048, 4096], P('section', 'tensor', 'dp')
- gain_grad: float32 [2, 4096], P('section', 'tensor')
All inputs are finite; a program needn't handle non-finite values.
Results may differ from a plain program's by a relative error of at most 0.0058.
The roundings to bfloat16 on the way count: a program that leaves them out, or rounds other values in their place, can miss the bound.
Values may be sent and summed in bfloat16 or wider, within the bound.
A program may use at most 192 MiB of HBM per device.

v0:
```python
import math
import jax
import jax.numpy as jnp
from jax import lax
from jax.sharding import PartitionSpec as P

HD = 128
KV = 8
HEADS = 16
EPS = 1e-05


def from_behind(value, axis, steps):
    count = lax.axis_size(axis)
    first, last = (max(0, -steps), min(count, count - steps))
    return lax.ppermute(value, axis, [(source, source + steps) for source in range(first, last)])


def attention_back(queries, saved_keys, saved_values, visible, attn_grad):
    score_scale = 1.0 / math.sqrt(HD)
    visible_full = visible[:, None, None, :, :]
    scores = (
        jnp.einsum("ibkgh,jbkh->bkgij", queries, saved_keys, preferred_element_type=jnp.float32)
        * score_scale
    )
    scores = jnp.where(visible_full, scores, -1e30)
    row_max = jnp.max(scores, axis=-1, keepdims=True)
    exp_scores = jnp.where(visible_full, jnp.exp(scores - row_max), 0.0)
    attn_probs = exp_scores / jnp.sum(exp_scores, axis=-1, keepdims=True)
    probs_bf16 = attn_probs.astype(jnp.bfloat16)
    attn_out = jnp.einsum(
        "bkgij,jbkh->ibkgh", probs_bf16, saved_values, preferred_element_type=jnp.float32
    ).astype(jnp.bfloat16)
    probs_grad = jnp.einsum(
        "ibkgh,jbkh->bkgij", attn_grad, saved_values, preferred_element_type=jnp.float32
    )
    row_dot = jnp.sum(attn_probs * probs_grad, axis=-1, keepdims=True)
    score_grad = (attn_probs * (probs_grad - row_dot) * score_scale).astype(jnp.bfloat16)
    query_grad = jnp.einsum(
        "bkgij,jbkh->ibkgh", score_grad, saved_keys, preferred_element_type=jnp.float32
    )
    key_grad = jnp.einsum(
        "bkgij,ibkgh->jbkh", score_grad, queries, preferred_element_type=jnp.float32
    )
    value_grad = jnp.einsum(
        "bkgij,ibkgh->jbkh", probs_bf16, attn_grad, preferred_element_type=jnp.float32
    )
    qkv_grads = jnp.concatenate(
        [query_grad, key_grad[..., None, :], value_grad[..., None, :]], axis=-2
    )
    return (attn_out, qkv_grads.astype(jnp.bfloat16))


def layer_back(
    inputs,
    upstream,
    queries,
    keys_local,
    values_local,
    segment_rows,
    gain_vec,
    weights_qkv,
    weights_out,
):
    seq_len, batch_count, local_width = inputs.shape
    inputs_full, upstream_full = (
        lax.all_gather(inputs, "tensor", axis=2, tiled=True),
        lax.all_gather(upstream, "tensor", axis=2, tiled=True),
    )
    model_width = inputs_full.shape[2]
    widened = inputs_full.astype(jnp.float32)
    root_mean = jnp.sqrt(jnp.mean(widened * widened, axis=-1, keepdims=True) + EPS)
    unit_rows = widened / root_mean
    normed_full = (unit_rows * gain_vec).astype(jnp.bfloat16)
    attn_grad = jnp.einsum(
        "ibd,cd->ibc", upstream_full, weights_out, preferred_element_type=jnp.float32
    ).astype(jnp.bfloat16)
    kv_local = keys_local.shape[-1] // HD
    group_size = HEADS // KV
    query_shape = (seq_len, batch_count, kv_local, group_size, HD)
    value_shape = (seq_len, batch_count, kv_local, HD)
    positions = jnp.arange(seq_len)
    causal = positions[None, :] <= positions[:, None]
    visible = (segment_rows[:, :, None] == segment_rows[:, None, :]) & causal[None]
    attn_out, qkv_grads = attention_back(
        queries.reshape(query_shape),
        keys_local.reshape(value_shape),
        values_local.reshape(value_shape),
        visible,
        attn_grad.reshape(query_shape),
    )
    attn_out = attn_out.reshape(seq_len, batch_count, -1)
    qkv_grads = qkv_grads.reshape(seq_len, batch_count, -1)
    grad_terms = jnp.einsum(
        "ibc,dc->ibd", qkv_grads, weights_qkv, preferred_element_type=jnp.float32
    )
    normed_grad = lax.psum_scatter(grad_terms, "tensor", scatter_dimension=2, tiled=True)
    first_col = lax.axis_index("tensor") * local_width
    unit_local = lax.dynamic_slice_in_dim(unit_rows, first_col, local_width, 2)
    gain_local = lax.dynamic_slice_in_dim(gain_vec, first_col, local_width, 0)
    scaled = normed_grad * gain_local
    row_part = jnp.sum(scaled * unit_local, axis=-1, keepdims=True)
    row_total = lax.psum(row_part, "tensor")
    through = (
        upstream.astype(jnp.float32) + (scaled - unit_local * (row_total / model_width)) / root_mean
    )
    gain_part = jnp.sum(normed_grad * unit_local, axis=(0, 1))
    return (
        through.astype(jnp.bfloat16),
        gain_part,
        normed_full,
        upstream_full,
        attn_out,
        qkv_grads,
    )


def shards(
    layer_input,
    norm_gain,
    upstream_grad,
    saved_queries,
    saved_keys,
    saved_values,
    segment_ids,
    batch_order,
    qkv_weight,
    out_weight,
):
    inputs = layer_input[0]
    upstream = upstream_grad[0]
    gain_vec = norm_gain[0]
    queries = saved_queries[0]
    keys_local = saved_keys[0]
    values_local = saved_values[0]
    id_rows = segment_ids[0]
    order_row = batch_order[0, 0]
    weights_qkv = qkv_weight[0]
    weights_out = out_weight[0]
    through, gain_part, normed_full, upstream_full, attn_out, qkv_grads = layer_back(
        inputs,
        upstream,
        queries,
        keys_local,
        values_local,
        id_rows,
        gain_vec,
        weights_qkv,
        weights_out,
    )
    ordered = jnp.take(through, order_row, axis=1)
    passed = from_behind(ordered, "section", -1)
    replicas = lax.axis_size("dp")
    qkv_total = jnp.einsum(
        "ibd,ibc->dc", normed_full, qkv_grads, preferred_element_type=jnp.float32
    )
    out_total = jnp.einsum(
        "ibc,ibd->cd", attn_out, upstream_full, preferred_element_type=jnp.float32
    )
    qkv_grad = lax.psum_scatter(qkv_total, "dp", scatter_dimension=0, tiled=True) / replicas
    out_grad = lax.psum_scatter(out_total, "dp", scatter_dimension=1, tiled=True) / replicas
    gain_grad = lax.psum(gain_part, "dp") / replicas
    return (passed[None], qkv_grad[None], out_grad[None], gain_grad[None])


def solution(mesh):
    placed = (
        P("section", "dp", None, "tensor"),
        P("section", None),
        P("section", "dp", None, "tensor"),
        P("section", "dp", None, "tensor"),
        P("section", "dp", None, "tensor"),
        P("section", "dp", None, "tensor"),
        P("section", None, "dp"),
        P("section", "dp", None),
        P("section", None, "tensor"),
        P("section", "tensor", None),
    )
    return jax.shard_map(
        shards,
        mesh=mesh,
        in_specs=placed,
        out_specs=(
            P("section", "dp", None, "tensor"),
            P("section", "dp", "tensor"),
            P("section", "tensor", "dp"),
            P("section", "tensor"),
        ),
        check_vma=False,
    )
```

profile of v0, /device:TPU:1, one launch (start us, length us, event | category | flops | bytes accessed | tf_op | source)
XLA Modules:
  0.0 406.7 jit_solution(5581653968323635845)
XLA Ops:
  7.2 0.0 all-gather.5.cloned.1.call-start
  7.2 2.5 copy.14
  9.8 0.0 all-gather.5.cloned.1.call-update
  9.8 0.0 all-gather.7.cloned.1.call-start
  9.9 1.2 copy.27
  11.1 0.0 reduce-scatter.4.cloned.1.call-start
  11.2 0.2 reshape_squeeze.9
  11.4 0.2 copy.36
  11.6 0.2 reshape_squeeze.11
  11.7 0.2 copy.45
  11.9 0.2 copy-done.4
  12.2 0.5 copy.54
  12.7 0.2 compare_and_fusion
  12.9 2.4 fusion.35
  15.3 46.4 %all-gather.5.cloned.1.call-done = bf16[1,256,2,4096]{3,1,2,0:T(8,128)(2,1)} async-done(((bf16[1,256,2,1024]{3,1,2,0:T(8,128)(2,1)}), bf16[1,256,2,4096]{3,1,2,0:T(8,128)(2,1)}) %all-gather.5.cloned.1.call-update) | async-done | bytes 4194320 | tf_op jit(solution)/shard_map/all_gather | solution.py:68
  61.7 5.8 %fusion.15 = bf16[256,2,512]{2,0,1:T(8,128)(2,1)S(1)} fusion(bf16[1,512,4096]{2,1,0:T(8,128)(2,1)} %param.19, bf16[1,256,2,4096]{3,1,2,0:T(8,128)(2,1)} %all-gather.5.cloned.1.call-done), kind=kOutput, calls=%fused_computation.30 | convolution fusion | flops 2147745792 | bytes 8912896 | tf_op jit(solution)/shard_map/ibd,cd->ibc/dot_general | solution.py:75
  67.5 0.2 copy.55
  67.7 0.5 fusion.36
  68.2 3.7 convolution_bitcast_fusion.4
  71.9 3.5 convolution_bitcast_fusion.2
  75.4 2.3 convolution_bitcast_fusion.3
  77.7 0.1 maximum_convert_fusion
  77.8 10.3 %fusion.3 = f32[256,2,4096]{2,0,1:T(8,128)} fusion(bf16[256,2,1024]{0,2,1:T(8,128)(2,1)S(1)} %bitcast.116, bf16[1,4096,1024]{2,1,0:T(8,128)(2,1)} %param.18), kind=kOutput, calls=%fused_computation.7 | convolution fusion | flops 4294967296 | bytes 17825792 | tf_op jit(solution)/shard_map/ibc,dc->ibd/dot_general | solution.py:94
  88.1 0.2 reduce-scatter.8.cloned.1.call-start
  88.4 2.1 convolution_convert_fusion
  90.5 0.8 copy-done.2
  91.2 5.6 %convolution_bitcast_fusion.1 = f32[512,4096]{1,0:T(8,128)} fusion(bf16[256,2,512]{0,2,1:T(8,128)(2,1)S(1)} %bitcast.121, bf16[1,256,2,4096]{3,1,2,0:T(8,128)(2,1)S(1)} %copy-done.2), kind=kOutput, calls=%fused_computation.10 | convolution fusion | flops 2147483648 | bytes 13107200 | tf_op jit(solution)/shard_map/ibc,ibd->cd/dot_general | solution.py:157
  96.8 0.0 reduce-scatter.6.cloned.1.call-start
  96.9 15.8 %all-gather.7.cloned.1.call-done = bf16[1,256,2,4096]{3,1,2,0:T(8,128)(2,1)} async-done(((bf16[1,256,2,1024]{3,1,2,0:T(8,128)(2,1)}), bf16[1,256,2,4096]{3,1,2,0:T(8,128)(2,1)}) %all-gather.7.cloned.1.call-update) | async-done | bytes 4194320 | tf_op jit(solution)/shard_map/all_gather | solution.py:67
  112.7 3.2 fusion.2
  115.9 0.2 copy-done
  116.1 8.5 %convolution_bitcast_fusion = f32[4096,1024]{1,0:T(8,128)} fusion(bf16[256,2,1024]{0,2,1:T(8,128)(2,1)S(1)} %bitcast.117, f32[4096]{0:T(1024)S(1)} %bitcast.129, bf16[1,256,2,4096]{3,1,2,0:T(8,128)(2,1)S(1)} %copy-done, f32[256,2]{0,1:T(2,128)S(1)} %add_sqrt_fusion), kind=kOutput, calls=%fused_computation.5 | convolution fusion | flops 4303355904 | bytes 22038528 | tf_op jit(solution)/shard_map/ibd,ibc->dc/dot_general | solution.py:154
  124.7 0.6 copy-done.11
  125.4 6.7 %convert_divide_fusion = f32[256,2,4096]{2,0,1:T(8,128)} fusion(bf16[1,256,2,4096]{3,1,2,0:T(8,128)(2,1)} %all-gather.7.cloned.1.call-done, f32[256,2]{0,1:T(2,128)S(1)} %add_sqrt_fusion), kind=kLoop, calls=%fused_computation.3 | loop fusion | flops 4194304 | bytes 12584960 | tf_op jit(solution)/shard_map/div | solution.py:73
  132.1 64.0 %reduce-scatter.4.cloned.1.call-done = f32[256,2,1024]{2,0,1:T(8,128)} async-done(((f32[256,2,4096]{2,0,1:T(8,128)}), f32[256,2,1024]{2,0,1:T(8,128)}) %reduce-scatter.4.cloned.1.call-update) | async-done | bytes 2097168 | tf_op jit(solution)/shard_map/reduce_scatter | solution.py:97
  196.1 2.9 multiply_reduce_fusion
  199.0 6.5 %psum.14 = f32[256,2,1]{0,1,2:T(2,128)S(1)} all-reduce(f32[256,2,1]{0,1,2:T(2,128)S(1)} %bitcast.126), channel_id=1, replica_groups=mesh['section'=2,'dp'=16,'tensor'=4] {'tensor'}, use_global_device_ids=true, to_apply=%region_6.7 | all-reduce | flops 512 | bytes 4096 | tf_op jit(solution)/shard_map/psum | solution.py:103
  205.5 2.3 fusion.10
  207.9 0.6 gather_fusion
  208.5 0.2 select_bitcast_fusion
  208.7 5.1 %collective-permute-start = (bf16[256,2,1024]{2,0,1:T(8,128)(2,1)S(1)}, bf16[256,2,1024]{2,0,1:T(8,128)(2,1)S(1)}, u32[]{:S(2)}, u32[]{:S(2)}) collective-permute-start(bf16[256,2,1024]{2,0,1:T(8,128)(2,1)S(1)} %select_bitcast_fusion), channel_id=1, source_target_pairs={{64,0},{65,1},{66,2},{67,3},{68,4},{69,5},{70,6},{71,7},{72,8},{73... | collective-permute-start | bytes 3145736 | tf_op jit(solution)/shard_map/ppermute | solution.py:16
  213.7 33.7 %psum.15 = f32[1024]{0:T(1024)S(1)} all-reduce(f32[1024]{0:T(1024)S(1)} %get-tuple-element.8), channel_id=1, replica_groups=mesh['section'=2,'dp'=16,'tensor'=4] {'dp'}, use_global_device_ids=true, to_apply=%region_10.11 | all-reduce | flops 1024 | bytes 8192 | tf_op jit(solution)/shard_map/psum | solution.py:162
  247.4 0.6 broadcast_multiply_fusion
  248.0 35.4 %reduce-scatter.8.cloned.1.call-done = f32[512,256]{1,0:T(8,128)} async-done(((f32[512,4096]{1,0:T(8,128)}), f32[512,256]{1,0:T(8,128)}) %reduce-scatter.8.cloned.1.call-update) | async-done | bytes 524304 | tf_op jit(solution)/shard_map/reduce_scatter | solution.py:161
  283.4 1.9 multiply_bitcast_fusion.1
  285.3 2.0 copy.32
  287.3 110.5 %reduce-scatter.6.cloned.1.call-done = f32[256,1024]{1,0:T(8,128)} async-done(((f32[4096,1024]{1,0:T(8,128)}), f32[256,1024]{1,0:T(8,128)}) %reduce-scatter.6.cloned.1.call-update) | async-done | bytes 1048592 | tf_op jit(solution)/shard_map/reduce_scatter | solution.py:160
  397.8 2.3 multiply_bitcast_fusion
  (32 shorter events, 0.2 us)
Async XLA Ops:
  7.2 2.7 copy-start.3
  7.2 54.5 %all-gather.5.cloned.1.call-start = ((), (), s32[]{:S(2)}) async-start(), calls=%async_computation.6 | async-start | bytes 5242880 | tf_op jit(solution)/shard_map/all_gather | solution.py:68
  9.8 1.4 copy-start.5
  9.8 1.8 copy-start.6
  9.8 102.9 %all-gather.7.cloned.1.call-start = ((), (), s32[]{:S(2)}) async-start(), calls=%async_computation.7 | async-start | bytes 5242880 | tf_op jit(solution)/shard_map/all_gather | solution.py:67
  11.1 1.0 copy-start.4
  11.1 1.6 copy-start.9
  11.1 185.0 %reduce-scatter.4.cloned.1.call-start = ((), (), s32[]{:S(2)}) async-start(), calls=%async_computation.3 | async-start | bytes 10485760 | tf_op jit(solution)/shard_map/reduce_scatter | solution.py:97
  11.6 3.7 copy-start.7
  75.4 2.3 copy-start.8
  88.1 195.3 %reduce-scatter.8.cloned.1.call-start = ((), (), s32[]{:S(2)}) async-start(), calls=%async_computation.5 | async-start | bytes 8912896 | tf_op jit(solution)/shard_map/reduce_scatter | solution.py:161
  88.4 2.9 copy-start.2
  96.8 19.1 %copy-start.10 = (f32[1,4096]{1,0:T(1,128)S(1)}, f32[1,4096]{1,0:T(1,128)}, u32[]{:S(2)}) copy-start(f32[1,4096]{1,0:T(1,128)} %param.11) | copy-start | bytes 49156
  96.8 301.0 %reduce-scatter.6.cloned.1.call-start = ((), (), s32[]{:S(2)}) async-start(), calls=%async_computation.4 | async-start | bytes 17825792 | tf_op jit(solution)/shard_map/reduce_scatter | solution.py:160
  112.7 3.4 copy-start
  124.7 0.7 copy-start.11
  196.1 9.4 %copy-start.1 = (f32[256,2,1024]{2,0,1:T(8,128)S(1)}, f32[256,2,1024]{2,0,1:T(8,128)}, u32[]{:S(2)}) copy-start(f32[256,2,1024]{2,0,1:T(8,128)} %reduce-scatter.4.cloned.1.call-done) | copy-start | bytes 6291460
  208.7 76.6 %collective-permute-start = (bf16[256,2,1024]{2,0,1:T(8,128)(2,1)S(1)}, bf16[256,2,1024]{2,0,1:T(8,128)(2,1)S(1)}, u32[]{:S(2)}, u32[]{:S(2)}) collective-permute-start(bf16[256,2,1024]{2,0,1:T(8,128)(2,1)S(1)} %select_bitcast_fusion), channel_id=1, source_target_pairs={{64,0},{65,1},{66,2},{67,3},{68,4},{69,5},{70,6},{71,7},{72,8},{73... | collective-permute-start | bytes 3145736 | tf_op jit(solution)/shard_map/ppermute | solution.py:16
Sparse Core Ops, SparseCore 0:
  10.2 51.4 all-gather.4
  63.9 48.6 all-gather.6
  115.2 80.9 reduce-scatter.3
  199.4 83.9 reduce-scatter.7
  286.7 111.1 reduce-scatter.5
where the time goes:
time: 407 us
  waiting for transfers between devices  272 us (67%)
  matrix products  44.6 us (11%)
  blocking collectives  40.2 us (10%)
  other arithmetic  20.5 us (5%)
  between operations  14 us (3%)
  local copies, waits for them, and re-layouts  9.74 us (2%)
  starting transfers between devices  5.44 us (1%)
    reduce_scatter x1, waiting for transfers between devices, shards(): lax.psum_scatter(qkv_total, 'dp', scatter_dimension=0, tiled=True)  110 us
    reduce_scatter x1, waiting for transfers between devices, layer_back(): lax.psum_scatter(grad_terms, 'tensor', scatter_dimension=2, tiled=True)  64 us
    all_gather x1, waiting for transfers between devices, layer_back(): lax.all_gather(upstream, 'tensor', axis=2, tiled=True)  46.4 us
    reduce_scatter x1, waiting for transfers between devices, shards(): lax.psum_scatter(out_total, 'dp', scatter_dimension=1, tiled=True)  35.4 us
    psum x1, blocking collectives, shards(): gain_grad = lax.psum(gain_part, 'dp') / replicas  33.7 us
    all_gather x1, waiting for transfers between devices, layer_back(): lax.all_gather(inputs, 'tensor', axis=2, tiled=True)  15.8 us
    dot_general x1, matrix products, layer_back(): jnp.einsum('ibc,dc->ibd', qkv_grads, weights_qkv, preferred_element_type=...  10.3 us
    dot_general x1, matrix products, shards(): jnp.einsum('ibd,ibc->dc', normed_full, qkv_grads, preferred_element_type=...  8.55 us
  transfers between devices with their start and end apart: 6, of which 5 were waited for; matrix products, arithmetic and copies ran while one was open for 17% of the time, Pallas kernels for 0%

commit v1 on v0

--- a/solution.py
+++ b/solution.py
@@ -64,7 +64,9 @@
 ):
     seq_len, batch_count, local_width = inputs.shape
     inputs_full, upstream_full = (
-        lax.all_gather(inputs, "tensor", axis=2, tiled=True),
+        jnp.concatenate(
+            lax.all_to_all(jnp.stack([inputs] * lax.axis_size("tensor")), "tensor", 0, 0), axis=2
+        ),
         lax.all_gather(upstream, "tensor", axis=2, tiled=True),
     )
     model_width = inputs_full.shape[2]

time: 407 us -> 426 us (1.047)
  blocking collectives: 40.2 us -> 136 us
  waiting for transfers between devices: 272 us -> 196 us
  local copies, waits for them, and re-layouts: 9.74 us -> 16.2 us
  other arithmetic: 20.5 us -> 15.1 us
    all_to_all x0 -> x1, blocking collectives: none -> 96 us  [layer_back(): lax.all_to_all(jnp.stack([inputs] * lax.axis_size('tensor')), 'tensor', 0...]
    reduce_scatter x1, waiting for transfers between devices: 64 us -> 2.16 us  [layer_back(): lax.psum_scatter(grad_terms, 'tensor', scatter_dimension=2, tiled=True)]
    all_gather x1 -> x0, waiting for transfers between devices: 15.8 us -> none  [layer_back(): lax.all_gather(inputs, 'tensor', axis=2, tiled=True)]
    div x1, other arithmetic: 6.71 us -> 1.48 us  [layer_back(): unit_rows = widened / root_mean]
    unnamed x27 -> x26, local copies, waits for them, and re-layouts: 7.72 us -> 11.7 us
  transfers between devices with their start and end apart: 6 -> 5, of which waited for: 5 -> 4; matrix products, arithmetic and copies ran while one was open for 17% -> 8% of each run, Pallas kernels for 0% -> 0%
where the time goes in v1:
time: 426 us
  waiting for transfers between devices  196 us (46%)
  blocking collectives  136 us (32%)
  matrix products  43 us (10%)
  local copies, waits for them, and re-layouts  16.2 us (4%)
  other arithmetic  15.1 us (4%)
  between operations  14 us (3%)
  starting transfers between devices  5.43 us (1%)
    reduce_scatter x1, waiting for transfers between devices, shards(): lax.psum_scatter(qkv_total, 'dp', scatter_dimension=0, tiled=True)  111 us
    all_to_all x1, blocking collectives, layer_back(): lax.all_to_all(jnp.stack([inputs] * lax.axis_size('tensor')), 'tensor', 0...  96 us
    all_gather x1, waiting for transfers between devices, layer_back(): lax.all_gather(upstream, 'tensor', axis=2, tiled=True)  47.8 us
    reduce_scatter x1, waiting for transfers between devices, shards(): lax.psum_scatter(out_total, 'dp', scatter_dimension=1, tiled=True)  35.6 us
    psum x1, blocking collectives, shards(): gain_grad = lax.psum(gain_part, 'dp') / replicas  33.7 us
    unnamed x26, local copies, waits for them, and re-layouts  11.7 us
    dot_general x1, matrix products, layer_back(): jnp.einsum('ibc,dc->ibd', qkv_grads, weights_qkv, preferred_element_type=...  10.3 us
  transfers between devices with their start and end apart: 5, of which 4 were waited for; matrix products, arithmetic and copies ran while one was open for 8% of the time, Pallas kernels for 0%

profile of v1, /device:TPU:1, one launch (start us, length us, event | category | flops | bytes accessed | tf_op | source)
XLA Modules:
  0.0 426.0 jit_solution(5343442801518033539)
XLA Ops:
  7.2 2.5 copy.33
  9.8 0.2 reshape_squeeze.9
  10.0 0.2 copy.56
  10.2 0.2 reshape_squeeze.11
  10.4 0.2 copy.65
  10.5 0.3 copy-done.4
  10.8 0.5 copy.74
  11.4 0.2 compare_and_fusion
  11.6 2.4 fusion.35
  13.9 47.8 %all-gather.3.cloned.1.call-done = bf16[1,256,2,4096]{3,1,2,0:T(8,128)(2,1)} async-done(((bf16[1,256,2,1024]{3,1,2,0:T(8,128)(2,1)}), bf16[1,256,2,4096]{3,1,2,0:T(8,128)(2,1)}) %all-gather.3.cloned.1.call-update) | async-done | bytes 4194320 | tf_op jit(solution)/shard_map/all_gather | solution.py:70
  61.7 5.8 %fusion.15 = bf16[256,2,512]{2,0,1:T(8,128)(2,1)S(1)} fusion(bf16[1,512,4096]{2,1,0:T(8,128)(2,1)} %param.19, bf16[1,256,2,4096]{3,1,2,0:T(8,128)(2,1)} %all-gather.3.cloned.1.call-done), kind=kOutput, calls=%fused_computation.31 | convolution fusion | flops 2147745792 | bytes 8912896 | tf_op jit(solution)/shard_map/ibd,cd->ibc/dot_general | solution.py:77
  67.5 0.2 copy.75
  67.8 0.5 fusion.36
  68.2 1.1 copy-done.11
  69.3 0.5 convolution_bitcast_fusion.3
  69.8 3.8 convolution_bitcast_fusion.4
  73.6 3.8 convolution_bitcast_fusion.2
  77.5 1.2 maximum_convert_fusion
  78.7 10.3 %fusion.3 = f32[256,2,4096]{2,0,1:T(8,128)} fusion(bf16[256,2,1024]{0,2,1:T(8,128)(2,1)S(1)} %bitcast.113, bf16[1,4096,1024]{2,1,0:T(8,128)(2,1)} %param.18), kind=kOutput, calls=%fused_computation.7 | convolution fusion | flops 4294967296 | bytes 17825792 | tf_op jit(solution)/shard_map/ibc,dc->ibd/dot_general | solution.py:96
  89.1 2.1 convolution_convert_fusion
  91.2 0.7 copy-done.2
  91.9 5.6 %convolution_bitcast_fusion.1 = f32[512,4096]{1,0:T(8,128)} fusion(bf16[256,2,512]{0,2,1:T(8,128)(2,1)S(1)} %bitcast.121, bf16[1,256,2,4096]{3,1,2,0:T(8,128)(2,1)S(1)} %copy-done.2), kind=kOutput, calls=%fused_computation.10 | convolution fusion | flops 2147483648 | bytes 13107200 | tf_op jit(solution)/shard_map/ibc,ibd->cd/dot_general | solution.py:159
  97.5 0.2 reduce-scatter.6.cloned.1.call-start
  97.7 1.2 copy-done.3
  98.9 0.3 copy.46
  99.2 0.5 stack.3
  99.7 96.0 %all_to_all.5 = bf16[4,256,2,1024]{3,1,2,0:T(8,128)(2,1)S(1)} all-to-all(bf16[4,256,2,1024]{3,1,2,0:T(8,128)(2,1)S(1)} %stack.3), channel_id=1, replica_groups=mesh['section'=2,'dp'=16,'tensor'=4] {'tensor'}, dimensions={0} | all-to-all | bytes 8388608 | tf_op jit(solution)/shard_map/all_to_all | solution.py:68
  195.8 1.1 convert_bitcast_fusion
  196.8 1.7 copy.76
  198.5 0.9 fusion.2
  199.4 1.5 broadcast_divide_fusion
  200.9 3.2 copy-done
  204.1 8.2 %convolution_bitcast_fusion = f32[4096,1024]{1,0:T(8,128)} fusion(bf16[256,2,1024]{0,2,1:T(8,128)(2,1)S(1)} %bitcast.114, f32[256,2,4096]{2,0,1:T(8,128)S(1)} %broadcast_divide_fusion, f32[4096]{0:T(1024)S(1)} %bitcast.124), kind=kOutput, calls=%fused_computation.5 | convolution fusion | flops 4299161600 | bytes 26230784 | tf_op jit(solution)/shard_map/ibd,ibc->dc/dot_general | solution.py:156
  212.4 0.6 copy-done.10
  213.0 2.2 reduce-scatter.4.cloned.1.call-done
  215.2 2.9 multiply_reduce_fusion
  218.1 6.5 %psum.14 = f32[256,2,1]{0,1,2:T(2,128)S(1)} all-reduce(f32[256,2,1]{0,1,2:T(2,128)S(1)} %bitcast.127), channel_id=1, replica_groups=mesh['section'=2,'dp'=16,'tensor'=4] {'tensor'}, use_global_device_ids=true, to_apply=%region_6.7 | all-reduce | flops 512 | bytes 4096 | tf_op jit(solution)/shard_map/psum | solution.py:105
  224.6 2.3 fusion.10
  226.9 0.6 gather_fusion
  227.6 0.2 select_bitcast_fusion
  227.7 5.1 %collective-permute-start = (bf16[256,2,1024]{2,0,1:T(8,128)(2,1)S(1)}, bf16[256,2,1024]{2,0,1:T(8,128)(2,1)S(1)}, u32[]{:S(2)}, u32[]{:S(2)}) collective-permute-start(bf16[256,2,1024]{2,0,1:T(8,128)(2,1)S(1)} %select_bitcast_fusion), channel_id=1, source_target_pairs={{64,0},{65,1},{66,2},{67,3},{68,4},{69,5},{70,6},{71,7},{72,8},{73... | collective-permute-start | bytes 3145736 | tf_op jit(solution)/shard_map/ppermute | solution.py:16
  232.8 33.7 %psum.15 = f32[1024]{0:T(1024)S(1)} all-reduce(f32[1024]{0:T(1024)S(1)} %get-tuple-element.12), channel_id=1, replica_groups=mesh['section'=2,'dp'=16,'tensor'=4] {'dp'}, use_global_device_ids=true, to_apply=%region_10.11 | all-reduce | flops 1024 | bytes 8192 | tf_op jit(solution)/shard_map/psum | solution.py:164
  266.5 0.6 broadcast_multiply_fusion
  267.1 35.6 %reduce-scatter.8.cloned.1.call-done = f32[512,256]{1,0:T(8,128)} async-done(((f32[512,4096]{1,0:T(8,128)}), f32[512,256]{1,0:T(8,128)}) %reduce-scatter.8.cloned.1.call-update) | async-done | bytes 524304 | tf_op jit(solution)/shard_map/reduce_scatter | solution.py:163
  302.7 1.9 multiply_bitcast_fusion.1
  304.6 2.0 copy.52
  306.6 110.5 %reduce-scatter.6.cloned.1.call-done = f32[256,1024]{1,0:T(8,128)} async-done(((f32[4096,1024]{1,0:T(8,128)}), f32[256,1024]{1,0:T(8,128)}) %reduce-scatter.6.cloned.1.call-update) | async-done | bytes 1048592 | tf_op jit(solution)/shard_map/reduce_scatter | solution.py:162
  417.1 2.3 multiply_bitcast_fusion
  (33 shorter events, 0.3 us)
Async XLA Ops:
  7.2 2.7 copy-start.6
  7.2 3.0 copy-start.7
  7.2 54.5 %all-gather.3.cloned.1.call-start = ((), (), s32[]{:S(2)}) async-start(), calls=%async_computation.7 | async-start | bytes 5242880 | tf_op jit(solution)/shard_map/all_gather | solution.py:70
  9.7 1.0 copy-start.4
  9.7 1.6 copy-start.9
  9.8 205.4 %reduce-scatter.4.cloned.1.call-start = ((), (), s32[]{:S(2)}) async-start(), calls=%async_computation.4 | async-start | bytes 10485760 | tf_op jit(solution)/shard_map/reduce_scatter | solution.py:99
  11.3 2.6 copy-start.5
  67.8 1.6 copy-start.11
  89.1 213.6 %reduce-scatter.8.cloned.1.call-start = ((), (), s32[]{:S(2)}) async-start(), calls=%async_computation.6 | async-start | bytes 8912896 | tf_op jit(solution)/shard_map/reduce_scatter | solution.py:163
  89.1 2.8 copy-start.2
  97.5 1.5 copy-start.3
  97.5 319.6 %reduce-scatter.6.cloned.1.call-start = ((), (), s32[]{:S(2)}) async-start(), calls=%async_computation.5 | async-start | bytes 17825792 | tf_op jit(solution)/shard_map/reduce_scatter | solution.py:162
  199.4 4.7 %copy-start.8 = (f32[1,4096]{1,0:T(1,128)S(1)}, f32[1,4096]{1,0:T(1,128)}, u32[]{:S(2)}) copy-start(f32[1,4096]{1,0:T(1,128)} %param.11) | copy-start | bytes 49156
  200.9 3.2 copy-start
  212.3 0.7 copy-start.10
  215.2 9.4 %copy-start.1 = (f32[256,2,1024]{2,0,1:T(8,128)S(1)}, f32[256,2,1024]{2,0,1:T(8,128)}, u32[]{:S(2)}) copy-start(f32[256,2,1024]{2,0,1:T(8,128)} %reduce-scatter.4.cloned.1.call-done) | copy-start | bytes 6291460
  227.7 76.8 %collective-permute-start = (bf16[256,2,1024]{2,0,1:T(8,128)(2,1)S(1)}, bf16[256,2,1024]{2,0,1:T(8,128)(2,1)S(1)}, u32[]{:S(2)}, u32[]{:S(2)}) collective-permute-start(bf16[256,2,1024]{2,0,1:T(8,128)(2,1)S(1)} %select_bitcast_fusion), channel_id=1, source_target_pairs={{64,0},{65,1},{66,2},{67,3},{68,4},{69,5},{70,6},{71,7},{72,8},{73... | collective-permute-start | bytes 3145736 | tf_op jit(solution)/shard_map/ppermute | solution.py:16
Sparse Core Ops, SparseCore 0:
  10.2 51.4 all-gather.2
  89.2 125.9 reduce-scatter.3
  218.6 84.0 reduce-scatter.7
  306.0 111.1 reduce-scatter.5
